TPU v7x, 128 devices: a whole 4x4x4 slice. The times are simulated.
128 devices in a mesh: tm: 8 (over y, core), height: 16 (over x, z).
Axes of the slice: x: 4, y: 4, z: 4, core: 2. Of those that a mesh axis runs over, the one named last changes fastest.
Arguments:
- stream: bfloat16 [8, 64, 160, 2240], P('tm', 'height'), may hold values from -6 to 6
- query_tokens: bfloat16 [8, 64, 160, 1120], P('tm', 'height'), may hold values from -6 to 6
- key_tokens: bfloat16 [8, 64, 160, 1120], P('tm', 'height'), may hold values from -6 to 6
- value_tokens: bfloat16 [8, 64, 160, 1120], P('tm', 'height'), may hold values from -12 to 12
- out_weight: bfloat16 [1120, 2240], replicated, may hold values from -0.1875 to 0.1875
- in_weight: bfloat16 [2240, 2, 2800], P(None, None, 'height'), may hold values from -0.125 to 0.125
- conv_weight: float32 [3, 3, 2, 2800], replicated, may hold values from -1.2 to 1.2
Outputs:
- attended: bfloat16 [8, 64, 160, 1120], P('tm', 'height')
- gated: bfloat16 [8, 64, 160, 2800], P('tm', 'height')
All inputs are finite; a program needn't handle non-finite values.
Results may differ from a plain program's by a relative error of at most 0.0074.
Values may be sent and summed in bfloat16 or wider, within the bound.
A program may use at most 128 MiB of HBM per device.

v0:
```python
import jax
import jax.numpy as jnp
from jax import lax
from jax.sharding import PartitionSpec as P

HD = 112


def cut_along(x, dim, devices):
    lengths = x.shape
    parts = x.reshape(*lengths[:dim], devices, lengths[dim] // devices, *lengths[dim + 1 :])
    return jnp.moveaxis(parts, dim, 0)


def sent_and_summed(x, axis, dim):
    parts = cut_along(x, dim, lax.axis_size(axis))
    arrived = lax.all_to_all(parts, axis, split_axis=0, concat_axis=0, tiled=True)
    return arrived.sum(axis=0)


def sent_together(arrays, axis, dim, along):
    widths = [a.shape[along] for a in arrays]
    both = jnp.concatenate(arrays, axis=along)
    out = sent_and_summed(both, axis, dim)
    return tuple(jnp.split(out, [sum(widths[:k]) for k in range(1, len(widths))], axis=along))


def collected_together(x, axis):
    leaves = jax.tree.leaves(x)
    turns = sorted(range(len(leaves)), key=lambda k: -leaves[k].size)
    width = (1, *leaves[turns[0]].shape)[-1]
    lines = [
        jnp.pad(leaves[k].reshape(-1), (0, -leaves[k].size % width)).reshape(-1, width)
        for k in turns
    ]
    both, at, found = (lax.all_gather(jnp.concatenate(lines), axis), 0, {})
    for k, line in zip(turns, lines):
        slab = both[:, at : at + len(line)].reshape(len(both), -1)
        found[k] = slab[:, : leaves[k].size].reshape(-1, *leaves[k].shape)
        at += len(line)
    numbers = iter(range(len(leaves)))
    return jax.tree.map(lambda _: found[next(numbers)], x)


def prefix(value, axis, join, neutral):
    count, mine = (lax.axis_size(axis), lax.axis_index(axis))
    pieces = collected_together(value, axis)
    total = jax.tree.map(
        lambda part, zero: jnp.full_like(part, 0) + jnp.asarray(zero, part.dtype), value, neutral
    )

    def turn(position, total):
        longer = join(total, jax.tree.map(lambda part: part[position], pieces))
        return jax.tree.map(lambda new, old: jnp.where(position < mine, new, old), longer, total)

    return lax.fori_loop(0, count - 1, turn, total)


def sent_to_all(x, axis):
    copies = jnp.broadcast_to(x, (lax.axis_size(axis), *x.shape))
    return lax.all_to_all(copies, axis, split_axis=0, concat_axis=0, tiled=True)


def laid_out(parts, dim):
    lengths = list(parts.shape[1:])
    lengths[dim] *= parts.shape[0]
    return jnp.moveaxis(parts, 0, dim).reshape(lengths)


def gathered_copies(x, axis, dim):
    parts = sent_to_all(x, axis)
    return laid_out(parts, dim)


def with_halo(x, sides, width):
    for axis, dim in sides:
        devices, length = (lax.axis_size(axis), x.shape[dim])
        up = [(i, (i + 1) % devices) for i in range(devices - 1)]
        down = [(j, i) for i, j in up]
        last = lax.slice_in_dim(x, length - width, length, axis=dim)
        leading = lax.slice_in_dim(x, 0, width, axis=dim)
        before = lax.ppermute(last, axis, up)
        after = lax.ppermute(leading, axis, down)
        x = jnp.concatenate([before, x, after], axis=dim)
    return x


def feature(array):
    wide = array.astype(jnp.float32)
    return jnp.where(wide > 0, wide + 1.0, jnp.exp(jnp.minimum(wide, 0.0)))


def depthwise(padded, kernel):
    rows = padded.shape[1] - 2
    columns = padded.shape[2] - 2
    total = jnp.zeros(padded.shape[:1] + (rows, columns) + padded.shape[3:], jnp.float32)
    for row_off in range(3):
        for col_off in range(3):
            total = (
                total
                + padded[:, row_off : row_off + rows, col_off : col_off + columns].astype(
                    jnp.float32
                )
                * kernel[row_off, col_off]
            )
    return (total[..., 0, :] * jax.nn.silu(total[..., 1, :])).astype(jnp.bfloat16)


def add_pair(earlier, later):
    return (earlier[0] + later[0], earlier[1] + later[1])


def local(stream, query_tokens, key_tokens, value_tokens, out_weight, in_weight, conv_weight):
    frames_dev, rows_dev, columns, head_cols = query_tokens.shape
    heads = head_cols // HD
    count_tok = rows_dev * columns
    highest = lax.Precision.HIGHEST
    query_map = feature(query_tokens).reshape(frames_dev, count_tok, heads, HD)
    key_map = feature(key_tokens).reshape(frames_dev, count_tok, heads, HD)
    value_map = value_tokens.astype(jnp.float32).reshape(frames_dev, count_tok, heads, HD)
    states = jnp.einsum("fnha,fnhb->fahb", key_map, value_map, precision=highest).reshape(
        frames_dev, HD, head_cols
    )
    norms = jnp.sum(key_map, axis=1).reshape(frames_dev, 1, head_cols)
    states, norms = sent_together((states, norms), "height", 2, 1)
    states = jnp.cumsum(states, axis=0)
    norms = jnp.cumsum(norms, axis=0)
    before = prefix(
        (states[-1], norms[-1]),
        "tm",
        add_pair,
        (jnp.zeros_like(states[-1]), jnp.zeros_like(norms[-1])),
    )
    states = states + before[0]
    norms = norms + before[1]
    states, norms = (gathered_copies(states, "height", 2), gathered_copies(norms, "height", 2))
    numerator = jnp.einsum(
        "fnha,fahb->fnhb", query_map, states.reshape(frames_dev, HD, heads, HD), precision=highest
    )
    denominator = jnp.einsum(
        "fnha,fha->fnh", query_map, norms.reshape(frames_dev, heads, HD), precision=highest
    )
    attended = (
        (numerator / denominator[..., None])
        .reshape(frames_dev, rows_dev, columns, head_cols)
        .astype(jnp.bfloat16)
    )
    project = jnp.dot(
        attended.reshape(-1, head_cols), out_weight, preferred_element_type=jnp.float32
    )
    mixed = (stream.astype(jnp.float32) + project.reshape(stream.shape)).astype(jnp.bfloat16)
    expanded = jnp.einsum(
        "frwd,djc->frwjc",
        mixed,
        lax.all_gather(in_weight, "height", axis=2, tiled=True),
        preferred_element_type=jnp.float32,
    ).astype(jnp.bfloat16)
    padded = with_halo(expanded, (("height", 1),), 1)
    padded = jnp.pad(padded, ((0, 0), (0, 0), (1, 1), (0, 0), (0, 0)))
    gated = depthwise(padded, conv_weight)
    return (attended, gated)


def solution(mesh):
    placed = (
        P("tm", "height", None, None),
        P("tm", "height", None, None),
        P("tm", "height", None, None),
        P("tm", "height", None, None),
        P(),
        P(None, None, "height"),
        P(),
    )
    return jax.shard_map(
        local,
        mesh=mesh,
        in_specs=placed,
        out_specs=(P("tm", "height", None, None), P("tm", "height", None, None)),
        check_vma=False,
    )
```

profile of v0, /device:TPU:0, one launch (start us, length us, event | category | flops | bytes accessed | tf_op | source)
XLA Modules:
  0.0 301.4 jit_solution(4351893791225012609)
XLA Ops:
  10.1 4.4 %reshape.183 = f32[640,10,112]{2,1,0:T(8,128)} reshape(f32[1,4,160,1120]{3,2,1,0:T(8,128)S(1)} %get-tuple-element.171) | data formatting | bytes 5734400 | tf_op jit(solution)/shard_map/reshape.1
  14.4 4.5 %reshape.184 = bf16[640,10,112]{2,1,0:T(8,128)(2,1)S(1)} reshape(bf16[1,4,160,1120]{3,2,1,0:T(8,128)(2,1)} %param.12) | data formatting | bytes 2867200 | tf_op jit(solution)/shard_map/reshape
  18.9 6.3 %fusion.32 = f32[1,112,10,112]{3,1,2,0:T(8,128)S(1)} fusion(bf16[640,10,112]{2,1,0:T(8,128)(2,1)S(1)} %reshape.184, f32[640,10,112]{2,1,0:T(8,128)} %reshape.183), kind=kOutput, calls=%fused_computation.47 | convolution fusion | flops 963379200 | bytes 4802560 | tf_op jit(solution)/shard_map/fnha,fnhb->fahb/dot_general | solution.py:121
  27.5 8.4 %all-to-all-start = ((f32[16,1,113,70]{2,1,3,0:T(1,128)}), f32[16,1,113,70]{2,1,3,0:T(1,128)S(1)}, u32[]{:S(2)}, u32[]{:S(2)}) async-start(f32[16,1,113,70]{2,1,3,0:T(1,128)} %copy.56), calls=%async_computation | async-start | bytes 1146880 | tf_op jit(solution)/shard_map/all_to_all | solution.py:17
  35.9 16.7 %all-to-all-done = f32[16,1,113,70]{2,1,3,0:T(1,128)S(1)} async-done(((f32[16,1,113,70]{2,1,3,0:T(1,128)}), f32[16,1,113,70]{2,1,3,0:T(1,128)S(1)}, u32[]{:S(2)}, u32[]{:S(2)}) %all-to-all-start) | async-done | bytes 506272 | tf_op jit(solution)/shard_map/all_to_all | solution.py:17
  53.2 13.5 %all-gather.1 = f32[8,113,70]{1,2,0:T(8,128)S(1)} all-gather(f32[1,113,70]{1,2,0:T(8,128)S(1)} %maximum_bitcast_fusion.1), channel_id=2, replica_groups=mesh['tm'=8,'height'=16] {'tm'}, dimensions={0}, use_global_device_ids=true | all-gather | bytes 284760 | tf_op jit(solution)/shard_map/all_gather | solution.py:36
  69.2 5.8 %all-to-all-start.2 = ((f32[16,1,1,70]{3,2,1,0:T(1,128)}), f32[16,1,1,70]{3,2,1,0:T(1,128)S(1)}, u32[]{:S(2)}, u32[]{:S(2)}) async-start(f32[16,1,1,70]{3,2,1,0:T(1,128)} %broadcast_in_dim.24), calls=%async_computation.2 | async-start | bytes 16384 | tf_op jit(solution)/shard_map/all_to_all | solution.py:61
  75.1 7.6 %all-to-all-done.2 = f32[16,1,1,70]{3,2,1,0:T(1,128)S(1)} async-done(((f32[16,1,1,70]{3,2,1,0:T(1,128)}), f32[16,1,1,70]{3,2,1,0:T(1,128)S(1)}, u32[]{:S(2)}, u32[]{:S(2)}) %all-to-all-start.2) | async-done | bytes 4512 | tf_op jit(solution)/shard_map/all_to_all | solution.py:61
  83.8 3.8 %all-to-all-start.1 = ((f32[16,1,112,70]{2,1,3,0:T(1,128)}), f32[16,1,112,70]{2,1,3,0:T(1,128)S(1)}, u32[]{:S(2)}, u32[]{:S(2)}) async-start(f32[16,1,112,70]{2,1,3,0:T(1,128)} %broadcast_in_dim.22), calls=%async_computation.1 | async-start | bytes 1146880 | tf_op jit(solution)/shard_map/all_to_all | solution.py:61
  89.6 4.4 %reshape.185 = f32[640,10,112]{2,1,0:T(8,128)} reshape(f32[1,4,160,1120]{3,2,1,0:T(8,128)S(1)} %fusion.27) | data formatting | bytes 5734400 | tf_op jit(solution)/shard_map/reshape.7
  94.0 8.1 %copy.73 = f32[640,10,112]{0,2,1:T(8,128)S(1)} copy(f32[640,10,112]{2,1,0:T(8,128)} %reshape.185) | data formatting | bytes 5734400 | tf_op jit(solution)/shard_map/reshape.7
  105.0 3.5 %fusion.29 = bf16[1,640,10,112]{1,3,2,0:T(8,128)(2,1)} fusion(f32[112,10,112]{0,2,1:T(8,128)S(1)} %bitcast.141, f32[640,10,112]{0,2,1:T(8,128)S(1)} %copy.73, f32[640,10]{0,1:T(8,128)S(1)} %bitcast.142), kind=kOutput, calls=%fused_computation.44 | convolution fusion | flops 964812800 | bytes 4828160 | tf_op jit(solution)/shard_map/fnha,fahb->fnhb/dot_general | solution.py:137
  108.5 4.9 %convert_element_type.85 = bf16[4,160,1120]{1,0,2:T(4,128)(2,1)S(1)} reshape(bf16[1,640,10,112]{1,3,2,0:T(8,128)(2,1)} %fusion.29) | data formatting | bytes 2867200 | tf_op jit(solution)/shard_map/convert_element_type | solution.py:146
  113.5 8.6 %fusion.20 = bf16[4,160,2240,1]{2,1,3,0:T(8,128)(2,1)} fusion(bf16[1120,2240]{1,0:T(8,128)(2,1)} %param.13, bf16[1,4,160,2240]{3,2,1,0:T(8,128)(2,1)} %param.9, bf16[4,160,1120]{1,0,2:T(4,128)(2,1)S(1)} %convert_element_type.85), kind=kOutput, calls=%fused_computation.36 | convolution fusion | flops 3215564800 | bytes 12185600 | tf_op jit(solution)/shard_map/dot_general | solution.py:148
  122.0 60.5 %all-gather.4.cloned.1.call-done = bf16[2240,2,2800]{0,1,2:T(2,128)(2,1)} async-done(((bf16[2240,2,175]{0,1,2:T(2,128)(2,1)}), bf16[2240,2,2800]{0,1,2:T(2,128)(2,1)}) %all-gather.4.cloned.1.call-update) | async-done | bytes 25088016 | tf_op jit(solution)/shard_map/all_gather | solution.py:155
  182.6 25.4 %fusion.15 = bf16[4,160,2,2800]{3,1,2,0:T(8,128)(2,1)} fusion(bf16[4,160,2240,1]{2,1,3,0:T(8,128)(2,1)} %fusion.20, bf16[2240,2,2800]{0,1,2:T(2,128)(2,1)} %all-gather.4.cloned.1.call-done), kind=kOutput, calls=%fused_computation.26 | convolution fusion | flops 16059904000 | bytes 35123200 | tf_op jit(solution)/shard_map/frwd,djc->frwjc/dot_general | solution.py:152
  208.0 4.1 %fusion.39 = (bf16[1,1,160,2,2800]{4,2,3,1,0:T(8,128)(2,1)}, bf16[1,1,160,2,2800]{4,2,3,1,0:T(8,128)(2,1)}) fusion(bf16[1,4,160,2,2800]{4,2,3,1,0:T(8,128)(2,1)} %bitcast.133), kind=kLoop, calls=%fused_computation.66 | loop fusion | bytes 7168000 | tf_op jit(solution)/shard_map/slice | solution.py:80
  212.2 4.3 %collective-permute-start = (bf16[1,1,160,2,2800]{4,2,3,1,0:T(8,128)(2,1)}, bf16[1,1,160,2,2800]{4,2,3,1,0:T(8,128)(2,1)}, u32[]{:S(2)}, u32[]{:S(2)}) collective-permute-start(bf16[1,1,160,2,2800]{4,2,3,1,0:T(8,128)(2,1)} %get-tuple-element.169), channel_id=1, source_target_pairs={{0,1},{1,2},{2,3},{3,4},{4,5},{5,6},{6,7},{7,8},{8,9},{9,10},{10,1... | collective-permute-start | bytes 5376008 | tf_op jit(solution)/shard_map/ppermute | solution.py:82
  217.8 5.2 %convert_element_type.83 = bf16[1,4,160,1120]{2,1,3,0:T(4,128)(2,1)S(1)} reshape(bf16[1,640,10,112]{1,3,2,0:T(8,128)(2,1)} %fusion.29) | data formatting | bytes 2867200 | tf_op jit(solution)/shard_map/convert_element_type | solution.py:146
  226.3 27.6 %collective-permute-done = bf16[1,1,160,2,2800]{4,2,3,1,0:T(8,128)(2,1)} collective-permute-done((bf16[1,1,160,2,2800]{4,2,3,1,0:T(8,128)(2,1)}, bf16[1,1,160,2,2800]{4,2,3,1,0:T(8,128)(2,1)}, u32[]{:S(2)}, u32[]{:S(2)}) %collective-permute-start) | collective-permute-done | bytes 1792032 | tf_op jit(solution)/shard_map/ppermute | solution.py:82
  253.9 5.3 %collective-permute-done.1 = bf16[1,1,160,2,2800]{4,2,3,1,0:T(8,128)(2,1)} collective-permute-done((bf16[1,1,160,2,2800]{4,2,3,1,0:T(8,128)(2,1)}, bf16[1,1,160,2,2800]{4,2,3,1,0:T(8,128)(2,1)}, u32[]{:S(2)}, u32[]{:S(2)}) %collective-permute-start.1) | collective-permute-done | bytes 1792032 | tf_op jit(solution)/shard_map/ppermute | solution.py:83
  259.3 9.2 %fusion.12 = bf16[1,6,162,2,2800]{4,2,3,1,0:T(8,128)(2,1)S(1)} fusion(bf16[1,1,160,2,2800]{4,2,3,1,0:T(8,128)(2,1)} %collective-permute-done.1, bf16[1,4,160,2,2800]{4,2,3,1,0:T(8,128)(2,1)} %bitcast.134, bf16[1,1,160,2,2800]{4,2,3,1,0:T(8,128)(2,1)} %collective-permute-done), kind=kLoop, calls=%fused_computation.19 | loop fusion | flops 65318400 | bytes 21638400 | tf_op jit(solution)/shard_map/concatenate | solution.py:84
  268.5 18.5 %fusion.7 = f32[1,4,160,2,2800]{4,2,3,1,0:T(8,128)} fusion(bf16[4,160,2,2800]{3,1,2,0:T(8,128)(2,1)} %fusion.15, bf16[1,6,162,2,2800]{4,2,3,1,0:T(8,128)(2,1)S(1)} %fusion.12, bf16[1,1,160,2,2800]{4,2,3,1,0:T(8,128)(2,1)} %collective-permute-done.1, bf16[1,4,160,2,2800]{4,2,3,1,0:T(8,128)(2,1)} %bitcast.135, ...), kind=kLoop, calls=%fused_computation.14 | loop fusion | flops 100352000 | bytes 75465600 | tf_op jit(solution)/shard_map/add | solution.py:100
  287.0 7.5 %fusion.14 = bf16[1,4,160,2800]{3,2,1,0:T(8,128)(2,1)} fusion(f32[1,4,160,2,2800]{4,2,3,1,0:T(8,128)} %fusion.7), kind=kLoop, calls=%fused_computation.23 | loop fusion | flops 10752000 | bytes 17920000 | tf_op jit(solution)/shard_map/convert_element_type | solution.py:106
  (63 shorter events, 19.9 us)
Async XLA Ops:
  7.2 175.4 %all-gather.4.cloned.1.call-start = ((), (), s32[]{:S(2)}) async-start(), calls=%async_computation.3 | async-start | bytes 27417600 | tf_op jit(solution)/shard_map/all_gather | solution.py:155
  27.5 25.1 %all-to-all-start = ((f32[16,1,113,70]{2,1,3,0:T(1,128)}), f32[16,1,113,70]{2,1,3,0:T(1,128)S(1)}, u32[]{:S(2)}, u32[]{:S(2)}) async-start(f32[16,1,113,70]{2,1,3,0:T(1,128)} %copy.56), calls=%async_computation | async-start | bytes 1146880 | tf_op jit(solution)/shard_map/all_to_all | solution.py:17
  69.2 13.5 %all-to-all-start.2 = ((f32[16,1,1,70]{3,2,1,0:T(1,128)}), f32[16,1,1,70]{3,2,1,0:T(1,128)S(1)}, u32[]{:S(2)}, u32[]{:S(2)}) async-start(f32[16,1,1,70]{3,2,1,0:T(1,128)} %broadcast_in_dim.24), calls=%async_computation.2 | async-start | bytes 16384 | tf_op jit(solution)/shard_map/all_to_all | solution.py:61
  83.8 21.2 %all-to-all-start.1 = ((f32[16,1,112,70]{2,1,3,0:T(1,128)}), f32[16,1,112,70]{2,1,3,0:T(1,128)S(1)}, u32[]{:S(2)}, u32[]{:S(2)}) async-start(f32[16,1,112,70]{2,1,3,0:T(1,128)} %broadcast_in_dim.22), calls=%async_computation.1 | async-start | bytes 1146880 | tf_op jit(solution)/shard_map/all_to_all | solution.py:61
  208.0 9.7 %copy-start = (f32[3,3,2,2800]{3,2,1,0:T(2,128)S(1)}, f32[3,3,2,2800]{3,2,1,0:T(2,128)}, u32[]{:S(2)}) copy-start(f32[3,3,2,2800]{3,2,1,0:T(2,128)} %param.15) | copy-start | bytes 604804
  212.2 41.7 %collective-permute-start = (bf16[1,1,160,2,2800]{4,2,3,1,0:T(8,128)(2,1)}, bf16[1,1,160,2,2800]{4,2,3,1,0:T(8,128)(2,1)}, u32[]{:S(2)}, u32[]{:S(2)}) collective-permute-start(bf16[1,1,160,2,2800]{4,2,3,1,0:T(8,128)(2,1)} %get-tuple-element.169), channel_id=1, source_target_pairs={{0,1},{1,2},{2,3},{3,4},{4,5},{5,6},{6,7},{7,8},{8,9},{9,10},{10,1... | collective-permute-start | bytes 5376008 | tf_op jit(solution)/shard_map/ppermute | solution.py:82
  216.4 42.8 %collective-permute-start.1 = (bf16[1,1,160,2,2800]{4,2,3,1,0:T(8,128)(2,1)}, bf16[1,1,160,2,2800]{4,2,3,1,0:T(8,128)(2,1)}, u32[]{:S(2)}, u32[]{:S(2)}) collective-permute-start(bf16[1,1,160,2,2800]{4,2,3,1,0:T(8,128)(2,1)} %get-tuple-element.170), channel_id=1, source_target_pairs={{1,0},{2,1},{3,2},{4,3},{5,4},{6,5},{7,6},{8,7},{9,8},{10,9},{11,1... | collective-permute-start | bytes 5376008 | tf_op jit(solution)/shard_map/ppermute | solution.py:83
Sparse Core Ops, SparseCore 0:
  10.1 172.4 all-gather.3
where the time goes:
time: 302 us; the launch traced here: 301 us
  waiting for transfers between devices  118 us (39%)
  matrix products  45.5 us (15%)
  local copies, waits for them, and re-layouts  44.6 us (15%)
  other arithmetic  41.3 us (14%)
  starting transfers between devices  23.5 us (8%)
  between operations  14.2 us (5%)
  blocking collectives  13.5 us (4%)
    all_gather x1, waiting for transfers between devices, local(): lax.all_gather(in_weight, 'height', axis=2, tiled=True)  60.5 us
    ppermute x1, waiting for transfers between devices, with_halo(): before = lax.ppermute(last, axis, up)  27.6 us
    dot_general x1, matrix products, local(): jnp.einsum('frwd,djc->frwjc', mixed, lax.all_gather(in_weight, 'height',...  25.4 us
    add x1, other arithmetic, depthwise(): total + padded[:, row_off:row_off + rows, col_off:col_off + columns].asty...  18.5 us
    another operation x4, local copies, waits for them, and re-layouts  17 us
    all_to_all x1, waiting for transfers between devices, sent_and_summed(): lax.all_to_all(parts, axis, split_axis=0, concat_axis=0, tiled=True)  16.7 us
    all_gather x1, blocking collectives, collected_together(): both, at, found = (lax.all_gather(jnp.concatenate(lines), axis), 0, {})  13.5 us
    convert_element_type x2, local copies, waits for them, and re-layouts, local(): attended = (numerator / denominator[..., None]).reshape(frames_dev, rows_...  10.1 us
  transfers between devices with their start and end apart: 6, of which 5 were waited for; matrix products, arithmetic and copies ran while one was open for 22% of the time, Pallas kernels for 0%

commit v1 on v0

--- a/solution.py
+++ b/solution.py
@@ -4,6 +4,12 @@
 from jax.sharding import PartitionSpec as P
 
 HD = 112
+
+
+def supply_all_the_map(u):
+    q_next = jnp.stack([u for _ in range(lax.axis_size("height"))], 0)
+    high = lax.all_to_all(q_next, axis_name="height", split_axis=0, concat_axis=0)
+    return jnp.concatenate(high, axis=2)
 
 
 def cut_along(x, dim, devices):
@@ -150,10 +156,7 @@
     )
     mixed = (stream.astype(jnp.float32) + project.reshape(stream.shape)).astype(jnp.bfloat16)
     expanded = jnp.einsum(
-        "frwd,djc->frwjc",
-        mixed,
-        lax.all_gather(in_weight, "height", axis=2, tiled=True),
-        preferred_element_type=jnp.float32,
+        "frwd,djc->frwjc", mixed, supply_all_the_map(in_weight), preferred_element_type=jnp.float32
     ).astype(jnp.bfloat16)
     padded = with_halo(expanded, (("height", 1),), 1)
     padded = jnp.pad(padded, ((0, 0), (0, 0), (1, 1), (0, 0), (0, 0)))

time: 302 us -> 677 us (2.24)
  waiting for transfers between devices: 118 us -> 474 us
  blocking collectives: 13.5 us -> 27.8 us
  local copies, waits for them, and re-layouts: 44.6 us -> 58.9 us
  between operations: 14.2 us -> 0.85 us
    all_to_all x0 -> x1, waiting for transfers between devices: none -> 424 us  [supply_all_the_map(): lax.all_to_all(q_next, axis_name='height', split_axis=0, concat_axis=0)]
    all_gather x1 -> x0, waiting for transfers between devices: 60.5 us -> none  [local(): lax.all_gather(in_weight, 'height', axis=2, tiled=True)]
    another operation x4 -> x5, local copies, waits for them, and re-layouts: 17 us -> 32.2 us
    all_to_all x0 -> x1, blocking collectives: none -> 14.4 us  [sent_to_all(): return lax.all_to_all(copies, axis, split_axis=0, concat_axis=0, tiled=True)]
  transfers between devices with their start and end apart: 6 -> 5, of which waited for: 5 -> 5; matrix products, arithmetic and copies ran while one was open for 22% -> 6% of each run, Pallas kernels for 0% -> 0%
where the time goes in v1:
time: 677 us
  waiting for transfers between devices  474 us (70%)
  local copies, waits for them, and re-layouts  58.9 us (9%)
  matrix products  45.2 us (7%)
  other arithmetic  41.4 us (6%)
  starting transfers between devices  28 us (4%)
  blocking collectives  27.8 us (4%)
    all_to_all x1, waiting for transfers between devices, supply_all_the_map(): lax.all_to_all(q_next, axis_name='height', split_axis=0, concat_axis=0)  424 us
    dot_general x1, matrix products, local(): jnp.einsum('frwd,djc->frwjc', mixed, supply_all_the_map(in_weight), prefe...  25.5 us
    ppermute x1, waiting for transfers between devices, with_halo(): before = lax.ppermute(last, axis, up)  24.9 us
    add x1, other arithmetic, depthwise(): total + padded[:, row_off:row_off + rows, col_off:col_off + columns].asty...  18.6 us
    another operation x4, local copies, waits for them, and re-layouts  16.8 us
    another operation x1, local copies, waits for them, and re-layouts, supply_all_the_map(): q_next = jnp.stack([u for _ in range(lax.axis_size('height'))], 0)  15.4 us
    all_to_all x1, blocking collectives, sent_to_all(): return lax.all_to_all(copies, axis, split_axis=0, concat_axis=0, tiled=True)  14.4 us
  transfers between devices with their start and end apart: 5, of which 5 were waited for; matrix products, arithmetic and copies ran while one was open for 6% of the time, Pallas kernels for 0%

profile of v1, /device:TPU:0, one launch (start us, length us, event | category | flops | bytes accessed | tf_op | source)
XLA Modules:
  0.0 676.6 jit_solution(9943038197410115243)
XLA Ops:
  2.8 4.3 reshape.193
  7.1 4.5 reshape.194
  11.6 6.3 fusion.31
  20.2 8.0 %all-to-all-start = ((f32[16,1,113,70]{2,1,3,0:T(1,128)}), f32[16,1,113,70]{2,1,3,0:T(1,128)S(1)}, u32[]{:S(2)}, u32[]{:S(2)}) async-start(f32[16,1,113,70]{2,1,3,0:T(1,128)} %copy.59), calls=%async_computation | async-start | bytes 1146880 | tf_op jit(solution)/shard_map/all_to_all | solution.py:23
  28.2 12.0 %all-to-all-done = f32[16,1,113,70]{2,1,3,0:T(1,128)S(1)} async-done(((f32[16,1,113,70]{2,1,3,0:T(1,128)}), f32[16,1,113,70]{2,1,3,0:T(1,128)S(1)}, u32[]{:S(2)}, u32[]{:S(2)}) %all-to-all-start) | async-done | bytes 506272 | tf_op jit(solution)/shard_map/all_to_all | solution.py:23
  40.8 13.4 %all-gather.1 = f32[8,113,70]{1,2,0:T(8,128)S(1)} all-gather(f32[1,113,70]{1,2,0:T(8,128)S(1)} %maximum_bitcast_fusion.1), channel_id=2, replica_groups=mesh['tm'=8,'height'=16] {'tm'}, dimensions={0}, use_global_device_ids=true | all-gather | bytes 284760 | tf_op jit(solution)/shard_map/all_gather | solution.py:42
  60.3 7.4 %all-to-all-done.2 = f32[16,1,1,70]{3,2,1,0:T(1,128)S(1)} async-done(((f32[16,1,1,70]{3,2,1,0:T(1,128)}), f32[16,1,1,70]{3,2,1,0:T(1,128)S(1)}, u32[]{:S(2)}, u32[]{:S(2)}) %all-to-all-start.2) | async-done | bytes 4512 | tf_op jit(solution)/shard_map/all_to_all | solution.py:67
  68.0 14.4 %all_to_all.20 = f32[16,1,112,70]{2,1,3,0:T(1,128)S(1)} all-to-all(f32[16,1,112,70]{2,1,3,0:T(1,128)S(1)} %broadcast_in_dim.22), channel_id=1, replica_groups=mesh['tm'=8,'height'=16] {'height'}, dimensions={0} | all-to-all | bytes 1003520 | tf_op jit(solution)/shard_map/all_to_all | solution.py:67
  82.4 15.4 %stack.2 = bf16[16,2240,2,175]{1,2,3,0:T(2,128)(2,1)} broadcast(bf16[2240,2,175]{0,1,2:T(2,128)(2,1)S(1)} %copy-done), dimensions={1,2,3} | broadcast | bytes 26656000 | tf_op jit(solution)/shard_map/stack | solution.py:10
  97.8 5.7 all-to-all-start.3
  105.6 4.3 reshape.195
  109.9 8.1 %copy.78 = f32[640,10,112]{0,2,1:T(8,128)S(1)} copy(f32[640,10,112]{2,1,0:T(8,128)} %reshape.195) | data formatting | bytes 5734400 | tf_op jit(solution)/shard_map/reshape.7
  124.4 4.9 convert_element_type.85
  129.3 8.3 %fusion.19 = bf16[4,160,2240,1]{2,1,3,0:T(8,128)(2,1)} fusion(bf16[1120,2240]{1,0:T(8,128)(2,1)} %param.13, bf16[1,4,160,2240]{3,2,1,0:T(8,128)(2,1)} %param.9, bf16[4,160,1120]{1,0,2:T(4,128)(2,1)S(1)} %convert_element_type.85), kind=kOutput, calls=%fused_computation.35 | convolution fusion | flops 3215564800 | bytes 12185600 | tf_op jit(solution)/shard_map/dot_general | solution.py:154
  137.6 424.4 %all-to-all-done.3 = bf16[16,2240,2,175]{1,2,3,0:T(2,128)(2,1)} async-done(((bf16[16,2240,2,175]{1,2,3,0:T(2,128)(2,1)}), bf16[16,2240,2,175]{1,2,3,0:T(2,128)(2,1)}, u32[]{:S(2)}, u32[]{:S(2)}) %all-to-all-start.3) | async-done | bytes 25088032 | tf_op jit(solution)/shard_map/all_to_all | solution.py:11
  562.1 25.5 %fusion.14 = bf16[4,160,2,2800]{3,1,2,0:T(8,128)(2,1)} fusion(bf16[4,160,2240,1]{2,1,3,0:T(8,128)(2,1)} %fusion.19, bf16[2240,2,2800,1]{0,1,2,3:T(2,128)(2,1)} %bitcast.26), kind=kOutput, calls=%fused_computation.25 | convolution fusion | flops 16059904000 | bytes 35123200 | tf_op jit(solution)/shard_map/frwd,djc->frwjc/dot_general | solution.py:158
  587.5 4.1 fusion.38
  591.7 9.5 %collective-permute-start = (bf16[1,1,160,2,2800]{4,2,3,1,0:T(8,128)(2,1)}, bf16[1,1,160,2,2800]{4,2,3,1,0:T(8,128)(2,1)}, u32[]{:S(2)}, u32[]{:S(2)}) collective-permute-start(bf16[1,1,160,2,2800]{4,2,3,1,0:T(8,128)(2,1)} %get-tuple-element.169), channel_id=1, source_target_pairs={{0,1},{1,2},{2,3},{3,4},{4,5},{5,6},{6,7},{7,8},{8,9},{9,10},{10,1... | collective-permute-start | bytes 5376008 | tf_op jit(solution)/shard_map/ppermute | solution.py:88
  602.5 5.2 convert_element_type.83
  611.1 24.9 %collective-permute-done = bf16[1,1,160,2,2800]{4,2,3,1,0:T(8,128)(2,1)} collective-permute-done((bf16[1,1,160,2,2800]{4,2,3,1,0:T(8,128)(2,1)}, bf16[1,1,160,2,2800]{4,2,3,1,0:T(8,128)(2,1)}, u32[]{:S(2)}, u32[]{:S(2)}) %collective-permute-start) | collective-permute-done | bytes 1792032 | tf_op jit(solution)/shard_map/ppermute | solution.py:88
  635.9 5.3 collective-permute-done.1
  641.2 9.2 %fusion.11 = bf16[1,6,162,2,2800]{4,2,3,1,0:T(8,128)(2,1)S(1)} fusion(bf16[1,1,160,2,2800]{4,2,3,1,0:T(8,128)(2,1)} %collective-permute-done.1, bf16[1,4,160,2,2800]{4,2,3,1,0:T(8,128)(2,1)} %bitcast.134, bf16[1,1,160,2,2800]{4,2,3,1,0:T(8,128)(2,1)} %collective-permute-done), kind=kLoop, calls=%fused_computation.18 | loop fusion | flops 65318400 | bytes 21638400 | tf_op jit(solution)/shard_map/concatenate | solution.py:90
  650.5 18.6 %fusion.6 = f32[1,4,160,2,2800]{4,2,3,1,0:T(8,128)} fusion(bf16[4,160,2,2800]{3,1,2,0:T(8,128)(2,1)} %fusion.14, bf16[1,6,162,2,2800]{4,2,3,1,0:T(8,128)(2,1)S(1)} %fusion.11, bf16[1,1,160,2,2800]{4,2,3,1,0:T(8,128)(2,1)} %collective-permute-done.1, bf16[1,4,160,2,2800]{4,2,3,1,0:T(8,128)(2,1)} %bitcast.135, ...), kind=kLoop, calls=%fused_computation.13 | loop fusion | flops 100352000 | bytes 75465600 | tf_op jit(solution)/shard_map/add | solution.py:106
  669.1 7.5 %fusion.13 = bf16[1,4,160,2800]{3,2,1,0:T(8,128)(2,1)} fusion(f32[1,4,160,2,2800]{4,2,3,1,0:T(8,128)} %fusion.6), kind=kLoop, calls=%fused_computation.22 | loop fusion | flops 10752000 | bytes 17920000 | tf_op jit(solution)/shard_map/convert_element_type | solution.py:112
  (64 shorter events, 25.4 us)
Async XLA Ops:
  18.2 64.2 %copy-start = (bf16[2240,2,175]{0,1,2:T(2,128)(2,1)S(1)}, bf16[2240,2,175]{0,1,2:T(2,128)(2,1)}, u32[]{:S(2)}) copy-start(bf16[2240,2,175]{0,1,2:T(2,128)(2,1)} %param.14) | copy-start | bytes 4704004
  20.2 20.0 %all-to-all-start = ((f32[16,1,113,70]{2,1,3,0:T(1,128)}), f32[16,1,113,70]{2,1,3,0:T(1,128)S(1)}, u32[]{:S(2)}, u32[]{:S(2)}) async-start(f32[16,1,113,70]{2,1,3,0:T(1,128)} %copy.59), calls=%async_computation | async-start | bytes 1146880 | tf_op jit(solution)/shard_map/all_to_all | solution.py:23
  56.7 11.0 %all-to-all-start.2 = ((f32[16,1,1,70]{3,2,1,0:T(1,128)}), f32[16,1,1,70]{3,2,1,0:T(1,128)S(1)}, u32[]{:S(2)}, u32[]{:S(2)}) async-start(f32[16,1,1,70]{3,2,1,0:T(1,128)} %broadcast_in_dim.24), calls=%async_computation.2 | async-start | bytes 16384 | tf_op jit(solution)/shard_map/all_to_all | solution.py:67
  97.8 464.3 %all-to-all-start.3 = ((bf16[16,2240,2,175]{1,2,3,0:T(2,128)(2,1)}), bf16[16,2240,2,175]{1,2,3,0:T(2,128)(2,1)}, u32[]{:S(2)}, u32[]{:S(2)}) async-start(bf16[16,2240,2,175]{1,2,3,0:T(2,128)(2,1)} %stack.2), calls=%async_computation.3 | async-start | bytes 51609600 | tf_op jit(solution)/shard_map/all_to_all | solution.py:11
  587.5 14.9 %copy-start.1 = (f32[3,3,2,2800]{3,2,1,0:T(2,128)S(1)}, f32[3,3,2,2800]{3,2,1,0:T(2,128)}, u32[]{:S(2)}) copy-start(f32[3,3,2,2800]{3,2,1,0:T(2,128)} %param.15) | copy-start | bytes 604804
  591.7 44.2 %collective-permute-start = (bf16[1,1,160,2,2800]{4,2,3,1,0:T(8,128)(2,1)}, bf16[1,1,160,2,2800]{4,2,3,1,0:T(8,128)(2,1)}, u32[]{:S(2)}, u32[]{:S(2)}) collective-permute-start(bf16[1,1,160,2,2800]{4,2,3,1,0:T(8,128)(2,1)} %get-tuple-element.169), channel_id=1, source_target_pairs={{0,1},{1,2},{2,3},{3,4},{4,5},{5,6},{6,7},{7,8},{8,9},{9,10},{10,1... | collective-permute-start | bytes 5376008 | tf_op jit(solution)/shard_map/ppermute | solution.py:88
  601.2 40.0 %collective-permute-start.1 = (bf16[1,1,160,2,2800]{4,2,3,1,0:T(8,128)(2,1)}, bf16[1,1,160,2,2800]{4,2,3,1,0:T(8,128)(2,1)}, u32[]{:S(2)}, u32[]{:S(2)}) collective-permute-start(bf16[1,1,160,2,2800]{4,2,3,1,0:T(8,128)(2,1)} %get-tuple-element.170), channel_id=1, source_target_pairs={{1,0},{2,1},{3,2},{4,3},{5,4},{6,5},{7,6},{8,7},{9,8},{10,9},{11,1... | collective-permute-start | bytes 5376008 | tf_op jit(solution)/shard_map/ppermute | solution.py:89
